TPU v7x, 256 devices: a whole 4x4x8 slice. The times are simulated.
256 devices in a mesh: feat: 4 (over y), node: 64 (over x, z, core).
Axes of the slice: x: 4, y: 4, z: 8, core: 2. Of those that a mesh axis runs over, the one named last changes fastest.
Arguments:
- features: bfloat16 [64, 768, 2048], P('node', 'feat'), may hold values from -6 to 6
- tiles: bfloat16 [64, 48, 128, 128], P('node'), may hold values from -0.3125 to 0.3125
- tile_rows: int32 [64, 48], P('node'), may hold values from 0 to 15, as said below
- tile_cols: int32 [64, 48], P('node'), may hold values from 0 to 31
- send_rows: int32 [64, 64, 32], P('node'), may hold values from 0 to 2047, as said below
- send_count: int32 [64, 64], P('node'), may hold values from 0 to 32, as said below
- w_neigh: bfloat16 [768, 1024], P('feat'), may hold values from -0.15625 to 0.15625
- w_self: bfloat16 [768, 1024], P('feat'), may hold values from -0.15625 to 0.15625
- cotangent: bfloat16 [64, 2048, 1024], P('node', 'feat'), may hold values from -16 to 16
Outputs:
- hidden: bfloat16 [64, 2048, 1024], P('node', 'feat')
- grad_features: bfloat16 [64, 768, 2048], P('node', 'feat')
- grad_neigh: float32 [768, 1024], P('feat')
- grad_self: float32 [768, 1024], P('feat')
Inputs may be any that keep to these rules, and one draw needn't show every extreme that they name: `tile_rows`: for each partition the first 16 tiles feed the row blocks 0, 1, 2 and so on in order, so that every block of rows has a tile. `send_rows`: rows may repeat within a list. `send_count`: A partition sends nothing to itself, and every partition fills all 32 slots toward at least one other partition.
All inputs are finite; a program needn't handle non-finite values.
Results may differ from a plain program's by a relative error of at most 0.0058.
Values may be sent and summed in bfloat16 or wider, within the bound.
A program may use at most 128 MiB of HBM per device.

v0:
```python
import jax
import jax.numpy as jnp
from jax import lax
from jax.sharding import PartitionSpec as P


def per_device(
    features, tiles, tile_rows, tile_cols, send_rows, send_count, w_neigh, w_self, cotangent
):
    own_cols = features[0]
    feat_dev, own_rows = own_cols.shape
    tile_vals = tiles[0]
    tile_side = tile_vals.shape[1]
    row_ids = tile_rows[0]
    col_ids = tile_cols[0]
    targets = send_rows[0]
    amounts = send_count[0]
    parts, slots = targets.shape
    live_slots = lax.broadcasted_iota(jnp.int32, (parts, slots), 1) < amounts[:, None]
    picked = jnp.take(own_cols, targets.reshape(-1), axis=1).reshape(feat_dev, parts, slots)
    picked = jnp.where(live_slots[None], picked, jnp.zeros((), own_cols.dtype))
    arrived = lax.all_to_all(picked, "node", split_axis=1, concat_axis=1, tiled=True)
    extended = jnp.concatenate([own_cols, arrived.reshape(feat_dev, parts * slots)], axis=1)
    col_blocks = extended.shape[1] // tile_side
    row_blocks = own_rows // tile_side
    gathered_cols = extended.reshape(feat_dev, col_blocks, tile_side)[:, col_ids, :]
    partial_sums = jnp.einsum(
        "fkj,kij->fki", gathered_cols, tile_vals, preferred_element_type=jnp.float32
    )
    row_onehot = (row_ids[:, None] == lax.broadcasted_iota(jnp.int32, (1, row_blocks), 1)).astype(
        jnp.float32
    )
    aggregated = jnp.einsum(
        "fki,kr->fri", partial_sums, row_onehot, precision=lax.Precision.HIGHEST
    )
    aggregated = aggregated.reshape(feat_dev, own_rows).astype(jnp.bfloat16)
    full_neigh, full_self = (
        lax.all_gather(w_neigh, "feat", axis=0, tiled=True),
        lax.all_gather(w_self, "feat", axis=0, tiled=True),
    )
    agg_rows, self_rows = (
        lax.all_to_all(aggregated, "feat", split_axis=1, concat_axis=0, tiled=True),
        lax.all_to_all(own_cols, "feat", split_axis=1, concat_axis=0, tiled=True),
    )
    first_dims = (((0,), (0,)), ((), ()))
    preact = lax.dot_general(agg_rows, full_neigh, first_dims, preferred_element_type=jnp.float32)
    preact = preact + lax.dot_general(
        self_rows, full_self, first_dims, preferred_element_type=jnp.float32
    )
    hidden = jax.nn.silu(preact).astype(jnp.bfloat16)
    gate_sig = jax.nn.sigmoid(preact)
    grad_pre = (
        cotangent[0].astype(jnp.float32) * gate_sig * (1.0 + preact * (1.0 - gate_sig))
    ).astype(jnp.bfloat16)
    grad_scale = float(own_rows * lax.axis_size("node")) ** (-0.5)
    last_dims = (((1,), (1,)), ((), ()))
    term_neigh = jnp.dot(agg_rows, grad_pre, preferred_element_type=jnp.float32)
    term_self = jnp.dot(self_rows, grad_pre, preferred_element_type=jnp.float32)
    share_neigh, share_self = (
        lax.psum_scatter(term_neigh, "feat", scatter_dimension=0, tiled=True),
        lax.psum_scatter(term_self, "feat", scatter_dimension=0, tiled=True),
    )
    total_neigh, total_self = lax.psum((share_neigh, share_self), "node")
    back_agg = lax.dot_general(
        full_neigh, grad_pre, last_dims, preferred_element_type=jnp.float32
    ).astype(jnp.bfloat16)
    back_self = lax.dot_general(
        full_self, grad_pre, last_dims, preferred_element_type=jnp.float32
    ).astype(jnp.bfloat16)
    grad_agg, grad_own = (
        lax.all_to_all(back_agg, "feat", split_axis=0, concat_axis=1, tiled=True),
        lax.all_to_all(back_self, "feat", split_axis=0, concat_axis=1, tiled=True),
    )
    grad_blocks = grad_agg.reshape(feat_dev, row_blocks, tile_side)[:, row_ids, :]
    spread = jnp.einsum("fki,kij->fkj", grad_blocks, tile_vals, preferred_element_type=jnp.float32)
    col_onehot = (col_ids[:, None] == lax.broadcasted_iota(jnp.int32, (1, col_blocks), 1)).astype(
        jnp.float32
    )
    grad_ext = jnp.einsum("fkj,kc->fcj", spread, col_onehot, precision=lax.Precision.HIGHEST)
    grad_ext = grad_ext.reshape(feat_dev, col_blocks * tile_side)
    outgoing = grad_ext[:, own_rows:].reshape(feat_dev, parts, slots)
    returned = lax.all_to_all(outgoing, "node", split_axis=1, concat_axis=1, tiled=True)
    returned = jnp.where(live_slots[None], returned, jnp.zeros((), returned.dtype))
    grad_cols = grad_ext[:, :own_rows] + grad_own.astype(jnp.float32)
    grad_cols = grad_cols.at[:, targets.reshape(-1)].add(returned.reshape(feat_dev, parts * slots))
    return (
        hidden[None],
        grad_cols.astype(jnp.bfloat16)[None],
        total_neigh * grad_scale,
        total_self * grad_scale,
    )


def solution(mesh):
    placed = (
        P("node", "feat", None),
        P("node", None, None, None),
        P("node", None),
        P("node", None),
        P("node", None, None),
        P("node", None),
        P("feat", None),
        P("feat", None),
        P("node", "feat", None),
    )
    return jax.shard_map(
        per_device,
        mesh=mesh,
        in_specs=placed,
        out_specs=(
            P("node", "feat", None),
            P("node", "feat", None),
            P("feat", None),
            P("feat", None),
        ),
        check_vma=False,
    )
```

profile of v0, /device:TPU:8, one launch (start us, length us, event | category | flops | bytes accessed | tf_op | source)
XLA Modules:
  0.0 419.9 jit_solution(5458794064605959569)
XLA Ops:
  7.2 0.0 all-gather.3.cloned.1.call-start
  7.2 0.7 all-gather.3.cloned.1.call-update
  7.9 0.8 copy.54
  8.7 0.7 compare_and_fusion
  9.4 0.1 reshape_squeeze.7
  9.5 1.4 copy.53
  11.0 0.1 copy.52
  11.1 9.1 %gather_fusion = bf16[2048,192]{1,0:T(8,128)(2,1)} fusion(bf16[192,2048]{0,1:T(8,128)(2,1)S(1)} %bitcast.96, s32[2048]{0:T(1024)S(1)} %broadcast_clamp_fusion), kind=kCustom, calls=%fused_computation | custom fusion | bytes 1581056 | tf_op jit(solution)/shard_map/jit(_take)/gather | solution.py:20
  20.2 0.1 iota_compare_fusion
  20.3 3.4 select_select_fusion
  23.7 11.9 %all-to-all-start = ((bf16[192,64,32]{0,2,1:T(8,128)(2,1)}), bf16[192,64,32]{0,2,1:T(8,128)(2,1)S(1)}, u32[]{:S(2)}, u32[]{:S(2)}) async-start(bf16[192,64,32]{0,2,1:T(8,128)(2,1)} %select_select_fusion), calls=%async_computation | async-start | bytes 2097152 | tf_op jit(solution)/shard_map/all_to_all | solution.py:22
  35.7 0.0 all-gather.5.cloned.1.call-start
  35.7 0.7 all-gather.5.cloned.1.call-update
  36.4 0.2 copy.72
  36.6 1.1 copy.55
  37.7 26.1 %all-to-all-done = bf16[192,64,32]{0,2,1:T(8,128)(2,1)S(1)} async-done(((bf16[192,64,32]{0,2,1:T(8,128)(2,1)}), bf16[192,64,32]{0,2,1:T(8,128)(2,1)S(1)}, u32[]{:S(2)}, u32[]{:S(2)}) %all-to-all-start) | async-done | bytes 786464 | tf_op jit(solution)/shard_map/all_to_all | solution.py:22
  63.8 1.2 copy.56
  65.1 1.5 pad_maximum_fusion
  66.6 2.4 gather_fusion.1
  69.0 2.8 fusion.8
  71.8 5.2 %fusion.26 = bf16[192,16,128]{2,1,0:T(8,128)(2,1)} fusion(f32[192,48,128]{2,0,1:T(8,128)S(1)} %fusion.8, s32[48]{0:T(128)S(1)} %bitcast.112), kind=kOutput, calls=%fused_computation.32 | convolution fusion | flops 226886400 | bytes 5505216 | tf_op jit(solution)/shard_map/fki,kr->fri/dot_general | solution.py:33
  77.0 1.8 convert_element_type.50
  78.9 1.0 copy.58
  79.9 4.9 %all-to-all-start.1 = ((bf16[192,4,512]{2,0,1:T(8,128)(2,1)}), bf16[192,4,512]{2,0,1:T(8,128)(2,1)S(1)}, u32[]{:S(2)}, u32[]{:S(2)}) async-start(bf16[192,4,512]{2,0,1:T(8,128)(2,1)} %copy.58), calls=%async_computation.1 | async-start | bytes 1572864 | tf_op jit(solution)/shard_map/all_to_all | solution.py:42
  84.8 1.4 all_to_all.58
  86.2 2.2 copy.59
  88.4 7.8 %all-to-all-done.1 = bf16[192,4,512]{2,0,1:T(8,128)(2,1)S(1)} async-done(((bf16[192,4,512]{2,0,1:T(8,128)(2,1)}), bf16[192,4,512]{2,0,1:T(8,128)(2,1)S(1)}, u32[]{:S(2)}, u32[]{:S(2)}) %all-to-all-start.1) | async-done | bytes 786464 | tf_op jit(solution)/shard_map/all_to_all | solution.py:42
  96.2 4.9 %all-to-all-start.2 = ((bf16[192,4,512]{2,0,1:T(8,128)(2,1)}), bf16[192,4,512]{2,0,1:T(8,128)(2,1)S(1)}, u32[]{:S(2)}, u32[]{:S(2)}) async-start(bf16[192,4,512]{2,0,1:T(8,128)(2,1)} %copy.59), calls=%async_computation.2 | async-start | bytes 1572864 | tf_op jit(solution)/shard_map/all_to_all | solution.py:43
  101.1 3.8 fusion.39
  104.9 6.8 %all-to-all-done.2 = bf16[192,4,512]{2,0,1:T(8,128)(2,1)S(1)} async-done(((bf16[192,4,512]{2,0,1:T(8,128)(2,1)}), bf16[192,4,512]{2,0,1:T(8,128)(2,1)S(1)}, u32[]{:S(2)}, u32[]{:S(2)}) %all-to-all-start.2) | async-done | bytes 786464 | tf_op jit(solution)/shard_map/all_to_all | solution.py:43
  111.7 5.1 %fusion.15 = (bf16[512,1024]{1,0:T(8,128)(2,1)S(1)}, bf16[1,512,1024]{2,1,0:T(8,128)(2,1)}) fusion(bf16[1,512,1024]{2,1,0:T(8,128)(2,1)} %param.17, f32[512,1024]{1,0:T(8,128)} %fusion.39, bf16[768,512]{1,0:T(8,128)(2,1)S(1)} %bitcast.103, bf16[768,1024]{1,0:T(8,128)(2,1)} %all-gather.5.cloned.1.call-done), kind=kOutput, calls=%fused_computation.17 | convolution fusion | flops 812122112 | bytes 7602176 | tf_op jit(solution)/shard_map/dot_general | solution.py:47
  116.8 1.0 copy-done.3
  117.9 2.7 fusion.40
  120.5 0.0 reduce-scatter.5.cloned.1.call-start
  120.6 1.1 copy-done.4
  121.7 2.7 convolution_bitcast_fusion
  124.5 2.4 fusion.24
  126.9 1.2 copy.60
  128.1 4.9 %all-to-all-start.3 = ((bf16[4,192,512]{2,1,0:T(8,128)(2,1)}), bf16[4,192,512]{2,1,0:T(8,128)(2,1)S(1)}, u32[]{:S(2)}, u32[]{:S(2)}) async-start(bf16[4,192,512]{2,1,0:T(8,128)(2,1)} %bitcast.108), calls=%async_computation.3 | async-start | bytes 1572864 | tf_op jit(solution)/shard_map/all_to_all | solution.py:71
  133.0 3.3 fusion.25
  136.4 2.3 copy.65
  138.7 14.1 %all-to-all-done.3 = bf16[4,192,512]{2,1,0:T(8,128)(2,1)S(1)} async-done(((bf16[4,192,512]{2,1,0:T(8,128)(2,1)}), bf16[4,192,512]{2,1,0:T(8,128)(2,1)S(1)}, u32[]{:S(2)}, u32[]{:S(2)}) %all-to-all-start.3) | async-done | bytes 786464 | tf_op jit(solution)/shard_map/all_to_all | solution.py:71
  152.8 5.6 %all-to-all-start.4 = ((bf16[4,192,512]{2,1,0:T(8,128)(2,1)}), bf16[4,192,512]{2,1,0:T(8,128)(2,1)}, u32[]{:S(2)}, u32[]{:S(2)}) async-start(bf16[4,192,512]{2,1,0:T(8,128)(2,1)} %bitcast.32), calls=%async_computation.4 | async-start | bytes 1572864 | tf_op jit(solution)/shard_map/all_to_all | solution.py:72
  158.4 0.6 copy.61
  159.0 1.2 reshape.163
  160.2 1.3 copy.62
  161.6 2.4 gather_fusion.2
  163.9 2.4 fusion.11
  166.3 6.5 %fusion.16 = f32[192,32,128]{2,1,0:T(8,128)} fusion(f32[192,48,128]{2,0,1:T(8,128)S(1)} %fusion.11, s32[48]{0:T(128)S(1)} %bitcast.113), kind=kOutput, calls=%fused_computation.20 | convolution fusion | flops 452986368 | bytes 7864512 | tf_op jit(solution)/shard_map/fkj,kc->fcj/dot_general | solution.py:79
  172.9 5.0 %copy.71 = f32[192,32,128]{0,2,1:T(8,128)} copy(f32[192,32,128]{2,1,0:T(8,128)} %fusion.16) | data formatting | bytes 6291456 | tf_op jit(solution)/shard_map/reshape | solution.py:80
  177.9 1.3 convert_bitcast_fusion
  179.2 1.8 copy.66
  181.0 5.3 %fusion.38 = (f32[192,2048]{0,1:T(8,128)}, f32[192,2048]{0,1:T(8,128)}) fusion(f32[192,4096]{0,1:T(8,128)} %bitcast.97, f32[192,4,512]{0,2,1:T(8,128)} %copy.66), kind=kLoop, calls=%fused_computation.56 | loop fusion | flops 393216 | bytes 7864320 | tf_op jit(solution)/shard_map/slice | solution.py:81
  186.3 7.1 %all-to-all-start.5 = ((f32[192,64,32]{0,2,1:T(8,128)}), f32[192,64,32]{0,2,1:T(8,128)}, u32[]{:S(2)}, u32[]{:S(2)}) async-start(f32[192,64,32]{0,2,1:T(8,128)} %bitcast.98), calls=%async_computation.5 | async-start | bytes 4194304 | tf_op jit(solution)/shard_map/all_to_all | solution.py:82
  193.4 0.3 all-reduce.3.cloned.1.call-start
  193.7 0.0 reduce-scatter.3.cloned.1.call-done
  193.7 21.2 %reduce-scatter.5.cloned.1.call-done = f32[192,1024]{1,0:T(8,128)} async-done(((f32[768,1024]{1,0:T(8,128)}), f32[192,1024]{1,0:T(8,128)}) %reduce-scatter.5.cloned.1.call-update) | async-done | bytes 786448 | tf_op jit(solution)/shard_map/reduce_scatter | solution.py:61
  215.0 29.5 %all-to-all-done.5 = f32[192,64,32]{0,2,1:T(8,128)} async-done(((f32[192,64,32]{0,2,1:T(8,128)}), f32[192,64,32]{0,2,1:T(8,128)}, u32[]{:S(2)}, u32[]{:S(2)}) %all-to-all-start.5) | async-done | bytes 1572896 | tf_op jit(solution)/shard_map/all_to_all | solution.py:82
  244.4 3.2 broadcast_select_fusion
  247.7 14.9 %scatter_fusion = f32[192,2048]{0,1:T(8,128)} fusion(f32[192,2048]{0,1:T(8,128)} %get-tuple-element.23, s32[2048]{0:T(1024)S(1)} %bitcast.111, f32[2048,192]{1,0:T(8,128)} %bitcast.100), kind=kCustom, calls=%fused_computation.3 | custom fusion | flops 393216 | bytes 4726784 | tf_op jit(solution)/shard_map/scatter-add | solution.py:85
  262.5 1.7 convert_bitcast_fusion.1
  264.2 1.2 copy.69
  265.5 145.1 %all-reduce.3.cloned.1.call-done = (f32[192,1024]{1,0:T(8,128)}, f32[192,1024]{1,0:T(8,128)}) async-done(((f32[192,1024]{1,0:T(8,128)}, f32[192,1024]{1,0:T(8,128)}), (f32[192,1024]{1,0:T(8,128)}, f32[192,1024]{1,0:T(8,128)})) %all-reduce.3.cloned.1.call-update) | async-done | bytes 1572880 | tf_op jit(solution)/shard_map/psum | solution.py:63
  410.6 2.8 broadcast_multiply_fusion
  (27 shorter events, 0.1 us)
Async XLA Ops:
  7.2 61.8 %copy-start = (bf16[1,48,128,128]{3,2,1,0:T(8,128)(2,1)S(1)}, bf16[1,48,128,128]{3,2,1,0:T(8,128)(2,1)}, u32[]{:S(2)}) copy-start(bf16[1,48,128,128]{3,2,1,0:T(8,128)(2,1)} %param.10) | copy-start | bytes 4718596
  7.2 94.0 %all-gather.3.cloned.1.call-start = ((), (), s32[]{:S(2)}) async-start(), calls=%async_computation.8 | async-start | bytes 1966080 | tf_op jit(solution)/shard_map/all_gather | solution.py:38
  11.1 9.1 %copy-start.7 = (s32[1,64]{1,0:T(1,128)S(1)}, s32[1,64]{1,0:T(1,128)}, u32[]{:S(2)}) copy-start(s32[1,64]{1,0:T(1,128)} %param.14) | copy-start | bytes 772
  20.2 16.2 %copy-start.6 = (s32[1,48]{1,0:T(1,128)S(1)}, s32[1,48]{1,0:T(1,128)}, u32[]{:S(2)}) copy-start(s32[1,48]{1,0:T(1,128)} %param.12) | copy-start | bytes 580
  20.3 16.2 %copy-start.1 = (bf16[1,192,2048]{2,1,0:T(8,128)(2,1)S(1)}, bf16[1,192,2048]{2,1,0:T(8,128)(2,1)}, u32[]{:S(2)}) copy-start(bf16[1,192,2048]{2,1,0:T(8,128)(2,1)} %param.9) | copy-start | bytes 2359300
  23.7 40.1 %all-to-all-start = ((bf16[192,64,32]{0,2,1:T(8,128)(2,1)}), bf16[192,64,32]{0,2,1:T(8,128)(2,1)S(1)}, u32[]{:S(2)}, u32[]{:S(2)}) async-start(bf16[192,64,32]{0,2,1:T(8,128)(2,1)} %select_select_fusion), calls=%async_computation | async-start | bytes 2097152 | tf_op jit(solution)/shard_map/all_to_all | solution.py:22
  35.7 76.1 %all-gather.5.cloned.1.call-start = ((), (), s32[]{:S(2)}) async-start(), calls=%async_computation.9 | async-start | bytes 1966080 | tf_op jit(solution)/shard_map/all_gather | solution.py:39
  69.0 2.8 copy-start.5
  77.0 7.7 %copy-start.2 = (bf16[1,192,2048]{2,1,0:T(8,128)(2,1)S(1)}, bf16[1,192,2048]{2,1,0:T(8,128)(2,1)}, u32[]{:S(2)}) copy-start(bf16[1,192,2048]{2,1,0:T(8,128)(2,1)} %param.9) | copy-start | bytes 2359300
  79.9 16.3 %all-to-all-start.1 = ((bf16[192,4,512]{2,0,1:T(8,128)(2,1)}), bf16[192,4,512]{2,0,1:T(8,128)(2,1)S(1)}, u32[]{:S(2)}, u32[]{:S(2)}) async-start(bf16[192,4,512]{2,0,1:T(8,128)(2,1)} %copy.58), calls=%async_computation.1 | async-start | bytes 1572864 | tf_op jit(solution)/shard_map/all_to_all | solution.py:42
  96.2 15.5 %all-to-all-start.2 = ((bf16[192,4,512]{2,0,1:T(8,128)(2,1)}), bf16[192,4,512]{2,0,1:T(8,128)(2,1)S(1)}, u32[]{:S(2)}, u32[]{:S(2)}) async-start(bf16[192,4,512]{2,0,1:T(8,128)(2,1)} %copy.59), calls=%async_computation.2 | async-start | bytes 1572864 | tf_op jit(solution)/shard_map/all_to_all | solution.py:43
  101.1 92.6 %reduce-scatter.3.cloned.1.call-start = ((), (), s32[]{:S(2)}) async-start(), calls=%async_computation.10 | async-start | bytes 3932160 | tf_op jit(solution)/shard_map/reduce_scatter | solution.py:60
  116.8 1.0 copy-start.3
  120.5 1.2 copy-start.4
  120.5 94.4 %reduce-scatter.5.cloned.1.call-start = ((), (), s32[]{:S(2)}) async-start(), calls=%async_computation.11 | async-start | bytes 3932160 | tf_op jit(solution)/shard_map/reduce_scatter | solution.py:61
  128.1 24.7 %all-to-all-start.3 = ((bf16[4,192,512]{2,1,0:T(8,128)(2,1)}), bf16[4,192,512]{2,1,0:T(8,128)(2,1)S(1)}, u32[]{:S(2)}, u32[]{:S(2)}) async-start(bf16[4,192,512]{2,1,0:T(8,128)(2,1)} %bitcast.108), calls=%async_computation.3 | async-start | bytes 1572864 | tf_op jit(solution)/shard_map/all_to_all | solution.py:71
  152.8 25.1 %all-to-all-start.4 = ((bf16[4,192,512]{2,1,0:T(8,128)(2,1)}), bf16[4,192,512]{2,1,0:T(8,128)(2,1)}, u32[]{:S(2)}, u32[]{:S(2)}) async-start(bf16[4,192,512]{2,1,0:T(8,128)(2,1)} %bitcast.32), calls=%async_computation.4 | async-start | bytes 1572864 | tf_op jit(solution)/shard_map/all_to_all | solution.py:72
  186.3 58.1 %all-to-all-start.5 = ((f32[192,64,32]{0,2,1:T(8,128)}), f32[192,64,32]{0,2,1:T(8,128)}, u32[]{:S(2)}, u32[]{:S(2)}) async-start(f32[192,64,32]{0,2,1:T(8,128)} %bitcast.98), calls=%async_computation.5 | async-start | bytes 4194304 | tf_op jit(solution)/shard_map/all_to_all | solution.py:82
  193.4 217.2 %all-reduce.3.cloned.1.call-start = ((), (), s32[]{:S(2)}) async-start(), calls=%async_computation.12 | async-start | bytes 3145728 | tf_op jit(solution)/shard_map/psum | solution.py:63
Sparse Core Ops, SparseCore 0:
  9.8 30.9 all-gather.2
  42.6 29.1 all-gather.4
  120.7 48.8 reduce-scatter.2
  172.0 42.9 reduce-scatter.4
  218.3 192.2 all-reduce.2
where the time goes:
time: 421 us; the launch traced here: 420 us
  waiting for transfers between devices  252 us (60%)
  local copies, waits for them, and re-layouts  41.9 us (10%)
  starting transfers between devices  39.8 us (9%)
  matrix products  37 us (9%)
  other arithmetic  35 us (8%)
  between operations  13.9 us (3%)
    psum x1, waiting for transfers between devices, per_device(): total_neigh, total_self = lax.psum((share_neigh, share_self), 'node')  145 us
    all_to_all x1, waiting for transfers between devices, per_device(): lax.all_to_all(outgoing, 'node', split_axis=1, concat_axis=1, tiled=True)  29.5 us
    all_to_all x1, waiting for transfers between devices, per_device(): lax.all_to_all(picked, 'node', split_axis=1, concat_axis=1, tiled=True)  26.1 us
    reduce_scatter x1, waiting for transfers between devices, per_device(): lax.psum_scatter(term_self, 'feat', scatter_dimension=0, tiled=True)  21.2 us
    scatter-add x1, other arithmetic, per_device(): grad_cols.at[:, targets.reshape(-1)]  14.9 us
    all_to_all x1, waiting for transfers between devices, per_device(): lax.all_to_all(back_agg, 'feat', split_axis=0, concat_axis=1, tiled=True)  14.1 us
    all_to_all x1, starting transfers between devices, per_device(): lax.all_to_all(picked, 'node', split_axis=1, concat_axis=1, tiled=True)  11.9 us
    gather x1, local copies, waits for them, and re-layouts, per_device(): jnp.take(own_cols, targets.reshape(-1), axis=1)  9.06 us
  transfers between devices with their start and end apart: 11, of which 7 were waited for; matrix products, arithmetic and copies ran while one was open for 24% of the time, Pallas kernels for 0%

commit v1 on v0

--- a/solution.py
+++ b/solution.py
@@ -79,7 +79,10 @@
     grad_ext = jnp.einsum("fkj,kc->fcj", spread, col_onehot, precision=lax.Precision.HIGHEST)
     grad_ext = grad_ext.reshape(feat_dev, col_blocks * tile_side)
     outgoing = grad_ext[:, own_rows:].reshape(feat_dev, parts, slots)
-    returned = lax.all_to_all(outgoing, "node", split_axis=1, concat_axis=1, tiled=True)
+    returned = jnp.concatenate(
+        lax.all_to_all(jnp.stack(jnp.split(outgoing, lax.axis_size("node"), axis=1)), "node", 0, 0),
+        1,
+    )
     returned = jnp.where(live_slots[None], returned, jnp.zeros((), returned.dtype))
     grad_cols = grad_ext[:, :own_rows] + grad_own.astype(jnp.float32)
     grad_cols = grad_cols.at[:, targets.reshape(-1)].add(returned.reshape(feat_dev, parts * slots))

time: 421 us -> 443 us (1.052)
  local copies, waits for them, and re-layouts: 41.9 us -> 80.9 us
  waiting for transfers between devices: 252 us -> 235 us
    unnamed x20 -> x87, local copies, waits for them, and re-layouts: 5.82 us -> 43.7 us
    all_to_all x1, waiting for transfers between devices: 29.5 us -> 53 us  [per_device(): lax.all_to_all(jnp.stack(jnp.split(outgoing, lax.axis_size('node'), axis=...]
    reduce_scatter x1, waiting for transfers between devices: 21.2 us -> 0.02 us  [per_device(): lax.psum_scatter(term_self, 'feat', scatter_dimension=0, tiled=True)]
    psum x1, waiting for transfers between devices: 145 us -> 128 us  [per_device(): total_neigh, total_self = lax.psum((share_neigh, share_self), 'node')]
  transfers between devices with their start and end apart: 11 -> 11, of which waited for: 7 -> 6; matrix products, arithmetic and copies ran while one was open for 24% -> 31% of each run, Pallas kernels for 0% -> 0%
where the time goes in v1:
time: 443 us; the launch traced here: 442 us
  waiting for transfers between devices  235 us (53%)
  local copies, waits for them, and re-layouts  80.9 us (18%)
  starting transfers between devices  40.3 us (9%)
  matrix products  37.9 us (9%)
  other arithmetic  34.1 us (8%)
  between operations  14 us (3%)
    psum x1, waiting for transfers between devices, per_device(): total_neigh, total_self = lax.psum((share_neigh, share_self), 'node')  128 us
    all_to_all x1, waiting for transfers between devices, per_device(): lax.all_to_all(jnp.stack(jnp.split(outgoing, lax.axis_size('node'), axis=...  53 us
    unnamed x87, local copies, waits for them, and re-layouts  43.7 us
    all_to_all x1, waiting for transfers between devices, per_device(): lax.all_to_all(picked, 'node', split_axis=1, concat_axis=1, tiled=True)  26.1 us
    scatter-add x1, other arithmetic, per_device(): grad_cols.at[:, targets.reshape(-1)]  15 us
    all_to_all x1, starting transfers between devices, per_device(): lax.all_to_all(picked, 'node', split_axis=1, concat_axis=1, tiled=True)  11.9 us
    all_to_all x1, waiting for transfers between devices, per_device(): lax.all_to_all(back_agg, 'feat', split_axis=0, concat_axis=1, tiled=True)  11.5 us
    gather x1, local copies, waits for them, and re-layouts, per_device(): jnp.take(own_cols, targets.reshape(-1), axis=1)  9.06 us
  transfers between devices with their start and end apart: 11, of which 6 were waited for; matrix products, arithmetic and copies ran while one was open for 31% of the time, Pallas kernels for 0%

profile of v1, /device:TPU:8, one launch (start us, length us, event | category | flops | bytes accessed | tf_op | source)
XLA Modules:
  0.0 442.2 jit_solution(13668486838258660233)
XLA Ops:
  7.2 0.7 all-gather.3.cloned.1.call-update
  7.9 1.4 copy.116
  9.7 9.1 %gather_fusion = bf16[2048,192]{1,0:T(8,128)(2,1)} fusion(bf16[192,2048]{0,1:T(8,128)(2,1)S(1)} %bitcast.358, s32[2048]{0:T(1024)S(1)} %broadcast_clamp_fusion), kind=kCustom, calls=%fused_computation | custom fusion | bytes 1581056 | tf_op jit(solution)/shard_map/jit(_take)/gather | solution.py:20
  18.9 3.4 select_select_fusion
  22.3 11.9 %all-to-all-start = ((bf16[192,64,32]{0,2,1:T(8,128)(2,1)}), bf16[192,64,32]{0,2,1:T(8,128)(2,1)S(1)}, u32[]{:S(2)}, u32[]{:S(2)}) async-start(bf16[192,64,32]{0,2,1:T(8,128)(2,1)} %select_select_fusion), calls=%async_computation | async-start | bytes 2097152 | tf_op jit(solution)/shard_map/all_to_all | solution.py:22
  34.3 0.7 all-gather.5.cloned.1.call-update
  35.2 1.1 copy.118
  36.3 26.1 %all-to-all-done = bf16[192,64,32]{0,2,1:T(8,128)(2,1)S(1)} async-done(((bf16[192,64,32]{0,2,1:T(8,128)(2,1)}), bf16[192,64,32]{0,2,1:T(8,128)(2,1)S(1)}, u32[]{:S(2)}, u32[]{:S(2)}) %all-to-all-start) | async-done | bytes 786464 | tf_op jit(solution)/shard_map/all_to_all | solution.py:22
  62.4 1.2 copy.119
  63.7 1.5 pad_maximum_fusion
  65.2 2.4 gather_fusion.1
  67.6 2.8 fusion.8
  70.4 5.2 %fusion.28 = bf16[192,16,128]{2,1,0:T(8,128)(2,1)} fusion(f32[192,48,128]{2,0,1:T(8,128)S(1)} %fusion.8, s32[48]{0:T(128)S(1)} %bitcast.437), kind=kOutput, calls=%fused_computation.35 | convolution fusion | flops 226886400 | bytes 5505216 | tf_op jit(solution)/shard_map/fki,kr->fri/dot_general | solution.py:33
  75.6 1.8 convert_element_type.50
  77.4 1.0 copy.121
  78.4 4.9 %all-to-all-start.1 = ((bf16[192,4,512]{2,0,1:T(8,128)(2,1)}), bf16[192,4,512]{2,0,1:T(8,128)(2,1)S(1)}, u32[]{:S(2)}, u32[]{:S(2)}) async-start(bf16[192,4,512]{2,0,1:T(8,128)(2,1)} %copy.121), calls=%async_computation.1 | async-start | bytes 1572864 | tf_op jit(solution)/shard_map/all_to_all | solution.py:42
  83.4 1.4 all_to_all.58
  84.8 2.2 copy.122
  87.0 7.8 %all-to-all-done.1 = bf16[192,4,512]{2,0,1:T(8,128)(2,1)S(1)} async-done(((bf16[192,4,512]{2,0,1:T(8,128)(2,1)}), bf16[192,4,512]{2,0,1:T(8,128)(2,1)S(1)}, u32[]{:S(2)}, u32[]{:S(2)}) %all-to-all-start.1) | async-done | bytes 786464 | tf_op jit(solution)/shard_map/all_to_all | solution.py:42
  94.8 4.9 %all-to-all-start.2 = ((bf16[192,4,512]{2,0,1:T(8,128)(2,1)}), bf16[192,4,512]{2,0,1:T(8,128)(2,1)S(1)}, u32[]{:S(2)}, u32[]{:S(2)}) async-start(bf16[192,4,512]{2,0,1:T(8,128)(2,1)} %copy.122), calls=%async_computation.2 | async-start | bytes 1572864 | tf_op jit(solution)/shard_map/all_to_all | solution.py:43
  99.7 3.8 fusion.41
  103.5 6.8 %all-to-all-done.2 = bf16[192,4,512]{2,0,1:T(8,128)(2,1)S(1)} async-done(((bf16[192,4,512]{2,0,1:T(8,128)(2,1)}), bf16[192,4,512]{2,0,1:T(8,128)(2,1)S(1)}, u32[]{:S(2)}, u32[]{:S(2)}) %all-to-all-start.2) | async-done | bytes 786464 | tf_op jit(solution)/shard_map/all_to_all | solution.py:43
  110.3 5.1 %fusion.15 = (bf16[512,1024]{1,0:T(8,128)(2,1)S(1)}, bf16[1,512,1024]{2,1,0:T(8,128)(2,1)}) fusion(bf16[1,512,1024]{2,1,0:T(8,128)(2,1)} %param.17, f32[512,1024]{1,0:T(8,128)} %fusion.41, bf16[768,512]{1,0:T(8,128)(2,1)S(1)} %bitcast.425, bf16[768,1024]{1,0:T(8,128)(2,1)} %all-gather.5.cloned.1.call-done), kind=kOutput, calls=%fused_computation.18 | convolution fusion | flops 812122112 | bytes 7602176 | tf_op jit(solution)/shard_map/dot_general | solution.py:47
  115.4 1.0 copy-done.3
  116.4 2.7 fusion.42
  119.1 1.2 copy-done.4
  120.3 3.3 fusion.26
  123.6 2.3 copy.123
  125.9 5.6 %all-to-all-start.3 = ((bf16[4,192,512]{2,1,0:T(8,128)(2,1)}), bf16[4,192,512]{2,1,0:T(8,128)(2,1)}, u32[]{:S(2)}, u32[]{:S(2)}) async-start(bf16[4,192,512]{2,1,0:T(8,128)(2,1)} %bitcast.431), calls=%async_computation.3 | async-start | bytes 1572864 | tf_op jit(solution)/shard_map/all_to_all | solution.py:71
  131.5 3.3 fusion.27
  134.9 2.3 copy.128
  137.2 2.7 convolution_bitcast_fusion
  139.9 11.5 %all-to-all-done.3 = bf16[4,192,512]{2,1,0:T(8,128)(2,1)} async-done(((bf16[4,192,512]{2,1,0:T(8,128)(2,1)}), bf16[4,192,512]{2,1,0:T(8,128)(2,1)}, u32[]{:S(2)}, u32[]{:S(2)}) %all-to-all-start.3) | async-done | bytes 786464 | tf_op jit(solution)/shard_map/all_to_all | solution.py:71
  151.4 5.6 %all-to-all-start.4 = ((bf16[4,192,512]{2,1,0:T(8,128)(2,1)}), bf16[4,192,512]{2,1,0:T(8,128)(2,1)}, u32[]{:S(2)}, u32[]{:S(2)}) async-start(bf16[4,192,512]{2,1,0:T(8,128)(2,1)} %bitcast.32), calls=%async_computation.4 | async-start | bytes 1572864 | tf_op jit(solution)/shard_map/all_to_all | solution.py:72
  157.1 1.8 copy.124
  159.3 2.4 gather_fusion.2
  161.7 2.4 fusion.11
  164.1 6.5 %fusion.18 = f32[192,32,128]{2,1,0:T(8,128)} fusion(f32[192,48,128]{2,0,1:T(8,128)S(1)} %fusion.11, s32[48]{0:T(128)S(1)} %bitcast.438), kind=kOutput, calls=%fused_computation.23 | convolution fusion | flops 452986368 | bytes 7864512 | tf_op jit(solution)/shard_map/fkj,kc->fcj/dot_general | solution.py:79
  170.7 5.0 %copy.134 = f32[192,32,128]{0,2,1:T(8,128)} copy(f32[192,32,128]{2,1,0:T(8,128)} %fusion.18) | data formatting | bytes 6291456 | tf_op jit(solution)/shard_map/reshape | solution.py:80
  175.6 1.3 convert_bitcast_fusion
  177.0 1.8 copy.129
  178.8 4.6 %fusion.40 = (f32[192,2048]{0,1:T(8,128)S(1)}, f32[192,2048]{0,1:T(8,128)}) fusion(f32[192,4096]{0,1:T(8,128)} %bitcast.359, f32[192,4,512]{0,2,1:T(8,128)} %copy.129), kind=kLoop, calls=%fused_computation.186 | loop fusion | flops 393216 | bytes 7864320 | tf_op jit(solution)/shard_map/slice | solution.py:81
  187.7 0.6 constant_dynamic-update-slice_fusion.56
  192.0 0.6 constant_dynamic-update-slice_fusion.49
  196.3 0.6 constant_dynamic-update-slice_fusion.42
  201.1 0.6 constant_dynamic-update-slice_fusion.34
  203.6 0.6 constant_dynamic-update-slice_fusion.30
  204.2 0.6 constant_dynamic-update-slice_fusion.29
  206.1 0.6 constant_dynamic-update-slice_fusion.26
  211.0 0.6 constant_dynamic-update-slice_fusion.18
  213.4 0.6 constant_dynamic-update-slice_fusion.14
  218.9 0.6 constant_dynamic-update-slice_fusion.5
  220.8 0.6 constant_dynamic-update-slice_fusion.2
  221.4 0.6 constant_dynamic-update-slice_fusion.1
  222.0 0.6 constant_dynamic-update-slice_fusion
  222.6 7.0 %all-to-all-start.5 = ((f32[64,192,1,32]{1,3,2,0:T(8,128)}), f32[64,192,1,32]{1,3,2,0:T(8,128)}, u32[]{:S(2)}, u32[]{:S(2)}) async-start(f32[64,192,1,32]{1,3,2,0:T(8,128)} %constant_dynamic-update-slice_fusion), calls=%async_computation.5 | async-start | bytes 4194304 | tf_op jit(solution)/shard_map/all_to_all | solution.py:83
  230.2 53.0 %all-to-all-done.5 = f32[64,192,1,32]{1,3,2,0:T(8,128)} async-done(((f32[64,192,1,32]{1,3,2,0:T(8,128)}), f32[64,192,1,32]{1,3,2,0:T(8,128)}, u32[]{:S(2)}, u32[]{:S(2)}) %all-to-all-start.5) | async-done | bytes 1572896 | tf_op jit(solution)/shard_map/all_to_all | solution.py:83
  283.3 3.2 bitcast_select_fusion
  286.5 15.0 %scatter_custom_fusion = f32[192,2048]{0,1:T(8,128)} fusion(f32[192,2048]{0,1:T(8,128)} %get-tuple-element.23, s32[2048]{0:T(1024)S(1)} %bitcast.434, f32[192,2048]{0,1:T(8,128)} %bitcast_select_fusion), kind=kCustom, calls=%fused_computation.19 | custom fusion | flops 393216 | bytes 3670016 | tf_op jit(solution)/shard_map/scatter-add | solution.py:88
  301.5 1.7 convert_bitcast_fusion.1
  303.2 1.2 copy.132
  304.5 128.0 %all-reduce.3.cloned.1.call-done = (f32[192,1024]{1,0:T(8,128)}, f32[192,1024]{1,0:T(8,128)}) async-done(((f32[192,1024]{1,0:T(8,128)}, f32[192,1024]{1,0:T(8,128)}), (f32[192,1024]{1,0:T(8,128)}, f32[192,1024]{1,0:T(8,128)})) %all-reduce.3.cloned.1.call-update) | async-done | bytes 1572880 | tf_op jit(solution)/shard_map/psum | solution.py:63
  432.5 2.2 broadcast_multiply_fusion.1
  434.7 1.0 broadcast_multiply_fusion
  (100 shorter events, 32.9 us)
Async XLA Ops:
  7.2 60.4 %copy-start = (bf16[1,48,128,128]{3,2,1,0:T(8,128)(2,1)S(1)}, bf16[1,48,128,128]{3,2,1,0:T(8,128)(2,1)}, u32[]{:S(2)}) copy-start(bf16[1,48,128,128]{3,2,1,0:T(8,128)(2,1)} %param.10) | copy-start | bytes 4718596
  7.2 2.2 copy-start.6
  7.2 92.5 %all-gather.3.cloned.1.call-start = ((), (), s32[]{:S(2)}) async-start(), calls=%async_computation.8 | async-start | bytes 1966080 | tf_op jit(solution)/shard_map/all_gather | solution.py:38
  9.7 9.1 %copy-start.7 = (s32[1,64]{1,0:T(1,128)S(1)}, s32[1,64]{1,0:T(1,128)}, u32[]{:S(2)}) copy-start(s32[1,64]{1,0:T(1,128)} %param.14) | copy-start | bytes 772
  18.8 16.2 %copy-start.8 = (s32[1,48]{1,0:T(1,128)S(1)}, s32[1,48]{1,0:T(1,128)}, u32[]{:S(2)}) copy-start(s32[1,48]{1,0:T(1,128)} %param.11) | copy-start | bytes 580
  18.9 16.2 %copy-start.9 = (s32[1,48]{1,0:T(1,128)S(1)}, s32[1,48]{1,0:T(1,128)}, u32[]{:S(2)}) copy-start(s32[1,48]{1,0:T(1,128)} %param.12) | copy-start | bytes 580
  18.9 16.2 %copy-start.1 = (bf16[1,192,2048]{2,1,0:T(8,128)(2,1)S(1)}, bf16[1,192,2048]{2,1,0:T(8,128)(2,1)}, u32[]{:S(2)}) copy-start(bf16[1,192,2048]{2,1,0:T(8,128)(2,1)} %param.9) | copy-start | bytes 2359300
  22.3 40.1 %all-to-all-start = ((bf16[192,64,32]{0,2,1:T(8,128)(2,1)}), bf16[192,64,32]{0,2,1:T(8,128)(2,1)S(1)}, u32[]{:S(2)}, u32[]{:S(2)}) async-start(bf16[192,64,32]{0,2,1:T(8,128)(2,1)} %select_select_fusion), calls=%async_computation | async-start | bytes 2097152 | tf_op jit(solution)/shard_map/all_to_all | solution.py:22
  34.2 76.1 %all-gather.5.cloned.1.call-start = ((), (), s32[]{:S(2)}) async-start(), calls=%async_computation.9 | async-start | bytes 1966080 | tf_op jit(solution)/shard_map/all_gather | solution.py:39
  75.6 7.8 %copy-start.2 = (bf16[1,192,2048]{2,1,0:T(8,128)(2,1)S(1)}, bf16[1,192,2048]{2,1,0:T(8,128)(2,1)}, u32[]{:S(2)}) copy-start(bf16[1,192,2048]{2,1,0:T(8,128)(2,1)} %param.9) | copy-start | bytes 2359300
  78.4 16.3 %all-to-all-start.1 = ((bf16[192,4,512]{2,0,1:T(8,128)(2,1)}), bf16[192,4,512]{2,0,1:T(8,128)(2,1)S(1)}, u32[]{:S(2)}, u32[]{:S(2)}) async-start(bf16[192,4,512]{2,0,1:T(8,128)(2,1)} %copy.121), calls=%async_computation.1 | async-start | bytes 1572864 | tf_op jit(solution)/shard_map/all_to_all | solution.py:42
  94.8 15.5 %all-to-all-start.2 = ((bf16[192,4,512]{2,0,1:T(8,128)(2,1)}), bf16[192,4,512]{2,0,1:T(8,128)(2,1)S(1)}, u32[]{:S(2)}, u32[]{:S(2)}) async-start(bf16[192,4,512]{2,0,1:T(8,128)(2,1)} %copy.122), calls=%async_computation.2 | async-start | bytes 1572864 | tf_op jit(solution)/shard_map/all_to_all | solution.py:43
  99.7 130.5 %reduce-scatter.3.cloned.1.call-start = ((), (), s32[]{:S(2)}) async-start(), calls=%async_computation.10 | async-start | bytes 3932160 | tf_op jit(solution)/shard_map/reduce_scatter | solution.py:60
  115.4 1.0 copy-start.3
  119.1 1.2 copy-start.4
  125.9 25.5 %all-to-all-start.3 = ((bf16[4,192,512]{2,1,0:T(8,128)(2,1)}), bf16[4,192,512]{2,1,0:T(8,128)(2,1)}, u32[]{:S(2)}, u32[]{:S(2)}) async-start(bf16[4,192,512]{2,1,0:T(8,128)(2,1)} %bitcast.431), calls=%async_computation.3 | async-start | bytes 1572864 | tf_op jit(solution)/shard_map/all_to_all | solution.py:71
  131.5 98.7 %reduce-scatter.5.cloned.1.call-start = ((), (), s32[]{:S(2)}) async-start(), calls=%async_computation.11 | async-start | bytes 3932160 | tf_op jit(solution)/shard_map/reduce_scatter | solution.py:61
  151.4 24.2 %all-to-all-start.4 = ((bf16[4,192,512]{2,1,0:T(8,128)(2,1)}), bf16[4,192,512]{2,1,0:T(8,128)(2,1)}, u32[]{:S(2)}, u32[]{:S(2)}) async-start(bf16[4,192,512]{2,1,0:T(8,128)(2,1)} %bitcast.32), calls=%async_computation.4 | async-start | bytes 1572864 | tf_op jit(solution)/shard_map/all_to_all | solution.py:72
  222.6 60.6 %all-to-all-start.5 = ((f32[64,192,1,32]{1,3,2,0:T(8,128)}), f32[64,192,1,32]{1,3,2,0:T(8,128)}, u32[]{:S(2)}, u32[]{:S(2)}) async-start(f32[64,192,1,32]{1,3,2,0:T(8,128)} %constant_dynamic-update-slice_fusion), calls=%async_computation.5 | async-start | bytes 4194304 | tf_op jit(solution)/shard_map/all_to_all | solution.py:83
  229.6 202.9 %all-reduce.3.cloned.1.call-start = ((), (), s32[]{:S(2)}) async-start(), calls=%async_computation.12 | async-start | bytes 3145728 | tf_op jit(solution)/shard_map/psum | solution.py:63
  432.5 2.2 copy-start.5
Sparse Core Ops, SparseCore 0:
  9.8 30.9 all-gather.2
  42.6 29.1 all-gather.4
  119.2 48.6 reduce-scatter.2
  170.3 43.0 reduce-scatter.4
  233.6 198.8 all-reduce.2
